TPU v7x, 32 devices: a whole 2x2x4 slice. The times are simulated.
32 devices in a mesh: kpt: 4 (over y, core), row: 4 (over z), col: 2 (over x).
Axes of the slice: x: 2, y: 2, z: 4, core: 2. Of those that a mesh axis runs over, the one named last changes fastest.
Arguments:
- a_matrix: bfloat16 [8, 4096, 4096], P('kpt', 'row', 'col'), parts along dimension 0, may hold values from -6 to 6
- b_matrix: bfloat16 [8, 4096, 4096], P('kpt', 'row', 'col'), parts along dimension 0, may hold values from -0.09375 to 0.09375
- a_level: int32 [128, 32], P('kpt'), parts along dimension 0, may hold values from 0 to 4, as said below
- b_level: int32 [128, 32], P('kpt'), parts along dimension 0, may hold values from 0 to 4, as said below
- limit: int32 [128, 32], P(('kpt', 'row'), 'col'), parts along dimension 0, may hold values from 3 to 8
Outputs:
- product: bfloat16 [8, 4096, 4096], P('kpt', 'row', 'col'), parts along dimension 0
- kept_count: int32 [128, 32], P(('kpt', 'row'), 'col'), parts along dimension 0
- kept_total: int32 [4], P('kpt'), parts along dimension 0
There are 4 independent parts, one for each index of `kpt`. A program takes and returns all parts, laid end to end along the dimension named above; each array names one. Nothing has to cross between parts.
Inputs may be any that keep to these rules, and one draw needn't show every extreme that they name: Each block's level is 0 (empty) or its norm exponent 1 to 4; the share of occupied blocks rises from some a sixth in the first block row of a_level (block column of b_level) to some six in seven in the last. `b_level`: as for a_level, with the share rising along block columns.
All inputs are finite; a program needn't handle non-finite values.
Results may differ from a plain program's by a relative error of at most 0.001.
Values may be sent and summed in bfloat16 or wider, within the bound.
No kernel may reach another device: no remote copies, remote signals or barrier semaphores. Data moves between devices by JAX's collectives and lax.ppermute only.
A program may use at most 576 MiB of HBM per device.

v0:
```python
import jax
import jax.numpy as jnp
from jax import lax
from jax.sharding import PartitionSpec as P

BLK = 128


def level_scale(levels):
    power = jnp.power(jnp.float32(2.0), (1 - levels).astype(jnp.float32))
    return jnp.where(levels > 0, power, jnp.float32(0.0))


def spread_blocks(small):
    return jnp.repeat(jnp.repeat(small, BLK, axis=0), BLK, axis=1)


def block_terms(a_piece, a_lev, b_piece, b_lev, limit):
    keep = (
        (a_lev[:, :, None] > 0)
        & (b_lev[None, :, :] > 0)
        & (a_lev[:, :, None] + b_lev[None, :, :] <= limit[:, None, :])
    )
    counted = jnp.sum(keep.astype(jnp.int32), axis=1)
    results = []
    for column in range(limit.shape[1]):
        mask = jnp.repeat(keep[:, :, column], BLK, axis=0)
        masked = jnp.where(mask[None], a_piece, jnp.zeros((), jnp.bfloat16))
        right = b_piece[:, :, column * BLK : (column + 1) * BLK]
        real_real = jnp.dot(masked[0], right[0], preferred_element_type=jnp.float32)
        imag_imag = jnp.dot(masked[1], right[1], preferred_element_type=jnp.float32)
        real_imag = jnp.dot(masked[0], right[1], preferred_element_type=jnp.float32)
        imag_real = jnp.dot(masked[1], right[0], preferred_element_type=jnp.float32)
        results.append(jnp.stack([real_real - imag_imag, real_imag + imag_real]))
    return (jnp.concatenate(results, axis=2), counted)


def shards(a_matrix, b_matrix, a_level, b_level, limit):
    row_place = lax.axis_index("row")
    col_place = lax.axis_index("col")
    row_blocks = a_matrix.shape[1] // BLK
    col_blocks = a_matrix.shape[2] // BLK
    a_own = lax.dynamic_slice(
        a_level, (row_place * row_blocks, col_place * col_blocks), (row_blocks, col_blocks)
    )
    b_own = lax.dynamic_slice(
        b_level, (row_place * row_blocks, col_place * col_blocks), (row_blocks, col_blocks)
    )
    a_eff = a_matrix * spread_blocks(level_scale(a_own)).astype(jnp.bfloat16)[None]
    b_eff = b_matrix * spread_blocks(level_scale(b_own)).astype(jnp.bfloat16)[None]
    a_band = lax.dynamic_slice_in_dim(a_level, row_place * row_blocks, row_blocks, 0)
    b_band = lax.dynamic_slice_in_dim(b_level, col_place * col_blocks, col_blocks, 1)
    a_levels = jnp.repeat(a_band, BLK, axis=1)
    b_levels = jnp.repeat(b_band, BLK, axis=0)
    a_whole = lax.all_gather(a_eff, "col", axis=2, tiled=True)
    added, counted = block_terms(
        a_whole, a_levels, lax.all_gather(b_eff, "row", axis=1, tiled=True), b_levels, limit
    )
    kept_count = counted // BLK
    kept_total = lax.psum(jnp.sum(kept_count).reshape(1), ("row", "col"))
    return (added.astype(jnp.bfloat16), kept_count, kept_total)


def solution(mesh):
    in_specs = (
        P("kpt", "row", "col"),
        P("kpt", "row", "col"),
        P("kpt", None),
        P("kpt", None),
        P(("kpt", "row"), "col"),
    )
    out_specs = (P("kpt", "row", "col"), P(("kpt", "row"), "col"), P("kpt"))
    return jax.shard_map(shards, mesh=mesh, in_specs=in_specs, out_specs=out_specs, check_vma=False)
```

profile of v0, /device:TPU:0, one launch (start us, length us, event | category | flops | bytes accessed | tf_op | source)
XLA Modules:
  0.0 1229.6 jit_solution(12622931891409190300)
XLA Ops:
  25.3 8.4 broadcast_multiply_fusion
  37.7 14.6 %psum.7 = s32[1]{0:T(128)} all-reduce(s32[1]{0:T(128)} %bitcast.131), channel_id=1, replica_groups=mesh['kpt'=4,'row'=4,'col'=2] {'row','col'}, use_global_device_ids=true, to_apply=%region_2.3 | all-reduce | flops 1 | bytes 8 | tf_op jit(solution)/shard_map/psum | solution.py:60
  52.3 168.1 %all-gather.3.cloned.1.call-done = bf16[2,1024,4096]{2,1,0:T(8,128)(2,1)} async-done(((bf16[2,1024,2048]{2,1,0:T(8,128)(2,1)}), bf16[2,1024,4096]{2,1,0:T(8,128)(2,1)}) %all-gather.3.cloned.1.call-update) | async-done | bytes 16777232 | tf_op jit(solution)/shard_map/all_gather | solution.py:55
  285.2 115.4 %broadcast_select_fusion = (bf16[2,1024,4096]{2,1,0:T(8,128)(2,1)}, bf16[2,1024,4096]{2,1,0:T(8,128)(2,1)}, bf16[2,1024,4096]{2,1,0:T(8,128)(2,1)}, bf16[2,1024,...) fusion(bf16[2,1024,4096]{2,1,0:T(8,128)(2,1)} %all-gather.3.clo, ...), kind=kLoop, calls=%fused_computation | loop fusion | flops 134217728 | bytes 352321536 | tf_op jit(solution)/shard_map/jit(_where)/select_n | solution.py:28
  400.6 382.8 %all-gather.5.cloned.1.call-done = bf16[2,4096,2048]{2,1,0:T(8,128)(2,1)} async-done(((bf16[2,1024,2048]{2,1,0:T(8,128)(2,1)}), bf16[2,4096,2048]{2,1,0:T(8,128)(2,1)}) %all-gather.5.cloned.1.call-update) | async-done | bytes 33554448 | tf_op jit(solution)/shard_map/all_gather | solution.py:57
  783.4 6.7 fusion.1
  811.6 6.5 fusion.4
  818.1 6.7 fusion.157
  824.8 6.5 fusion.158
  838.6 6.5 fusion.8
  845.2 6.5 fusion.155
  851.7 6.5 fusion.156
  859.0 6.7 fusion.13
  865.8 6.5 fusion.12
  872.3 6.5 fusion.153
  878.8 6.5 fusion.154
  892.6 6.5 fusion.16
  899.2 6.9 fusion.151
  906.1 6.5 fusion.152
  919.9 6.5 fusion.20
  926.5 6.5 fusion.149
  933.0 6.5 fusion.150
  940.3 6.7 fusion.25
  947.0 6.5 fusion.24
  953.5 6.5 fusion.147
  960.0 6.5 fusion.148
  973.9 6.5 fusion.28
  980.4 6.7 fusion.145
  987.1 6.5 fusion.146
  1001.0 6.5 fusion.32
  1007.5 6.5 fusion.143
  1021.3 6.9 fusion.37
  1028.2 6.5 fusion.36
  1034.7 6.5 fusion.141
  1055.1 6.5 fusion.40
  1061.7 6.7 fusion.139
  1082.2 6.5 fusion.44
  1088.7 6.5 fusion.137
  1102.6 6.7 fusion.49
  1109.3 6.5 fusion.48
  1115.8 6.5 fusion.135
  1136.2 6.5 fusion.52
  1142.7 6.9 fusion.133
  1163.4 6.5 fusion.56
  1170.0 6.5 fusion.131
  1190.3 6.7 fusion.60
  1197.0 6.5 fusion.129
  1210.9 11.6 copy.28
  (88 shorter events, 237.9 us)
Async XLA Ops:
  7.2 213.3 %all-gather.3.cloned.1.call-start = ((), (), s32[]{:S(2)}) async-start(), calls=%async_computation | async-start | bytes 25165824 | tf_op jit(solution)/shard_map/all_gather | solution.py:55
  7.2 7.6 copy-start.1
  18.6 764.8 %all-gather.5.cloned.1.call-start = ((), (), s32[]{:S(2)}) async-start(), calls=%async_computation.1 | async-start | bytes 41943040 | tf_op jit(solution)/shard_map/all_gather | solution.py:57
  25.3 8.4 copy-start.2
  25.3 9.6 copy-start.3
  783.4 8.5 copy-start
Sparse Core Ops, SparseCore 0:
  18.7 201.6 all-gather.2
  222.0 561.3 all-gather.4
where the time goes:
time: 1240 us; the launch traced here: 1230 us
  waiting for transfers between devices  551 us (44%)
  matrix products  412 us (33%)
  other arithmetic  144 us (12%)
  local copies, waits for them, and re-layouts  92.9 us (7%)
  between operations  14.8 us (1%)
  blocking collectives  14.6 us (1%)
    all_gather x1, waiting for transfers between devices, shards(): lax.all_gather(b_eff, 'row', axis=1, tiled=True)  383 us
    all_gather x1, waiting for transfers between devices, shards(): a_whole = lax.all_gather(a_eff, 'col', axis=2, tiled=True)  168 us
    select_n x1, other arithmetic, block_terms(): masked = jnp.where(mask[None], a_piece, jnp.zeros((), jnp.bfloat16))  115 us
    dot_general x16, matrix products, block_terms(): real_real = jnp.dot(masked[0], right[0], preferred_element_type=jnp.float32)  105 us
    dot_general x16, matrix products, block_terms(): imag_imag = jnp.dot(masked[1], right[1], preferred_element_type=jnp.float32)  103 us
    dot_general x16, matrix products, block_terms(): real_imag = jnp.dot(masked[0], right[1], preferred_element_type=jnp.float32)  102 us
    dot_general x16, matrix products, block_terms(): imag_real = jnp.dot(masked[1], right[0], preferred_element_type=jnp.float32)  102 us
    broadcast_in_dim x16, local copies, waits for them, and re-layouts, block_terms(): mask = jnp.repeat(keep[:, :, column], BLK, axis=0)  64.8 us
  transfers between devices with their start and end apart: 2, of which 2 were waited for; matrix products, arithmetic and copies ran while one was open for 16% of the time, Pallas kernels for 0%

commit v1 on v0

--- a/solution.py
+++ b/solution.py
@@ -52,7 +52,15 @@
     b_band = lax.dynamic_slice_in_dim(b_level, col_place * col_blocks, col_blocks, 1)
     a_levels = jnp.repeat(a_band, BLK, axis=1)
     b_levels = jnp.repeat(b_band, BLK, axis=0)
-    a_whole = lax.all_gather(a_eff, "col", axis=2, tiled=True)
+    ways, here = (lax.axis_size("col"), lax.axis_index("col"))
+    grown, reach = (a_eff, 1)
+    while reach < ways:
+        theirs = lax.ppermute(grown, "col", [(d, d ^ reach) for d in range(ways)])
+        mine_first = jnp.concatenate([grown, theirs], axis=2)
+        theirs_first = jnp.concatenate([theirs, grown], axis=2)
+        grown = jnp.where(here & reach == 0, mine_first, theirs_first)
+        reach = 2 * reach
+    a_whole = grown
     added, counted = block_terms(
         a_whole, a_levels, lax.all_gather(b_eff, "row", axis=1, tiled=True), b_levels, limit
     )

time: 1240 us -> 951 us (0.77)
  waiting for transfers between devices: 551 us -> 129 us
  blocking collectives: 14.6 us -> 205 us
  matrix products: 412 us -> 326 us
  other arithmetic: 144 us -> 205 us
  local copies, waits for them, and re-layouts: 92.9 us -> 58.1 us
    all_gather x1, waiting for transfers between devices: 383 us -> 129 us  [shards(): lax.all_gather(b_eff, 'row', axis=1, tiled=True)]
    psum x1, blocking collectives: 14.6 us -> 205 us  [shards(): kept_total = lax.psum(jnp.sum(kept_count).reshape(1), ('row', 'col'))]
    all_gather x1 -> x0, waiting for transfers between devices: 168 us -> none  [shards(): a_whole = lax.all_gather(a_eff, 'col', axis=2, tiled=True)]
    select_n x1 -> x6, other arithmetic: 115 us -> 176 us  [block_terms(): masked = jnp.where(mask[None], a_piece, jnp.zeros((), jnp.bfloat16))]
    dot_general x16, matrix products: 103 us -> 68.5 us  [block_terms(): imag_imag = jnp.dot(masked[1], right[1], preferred_element_type=jnp.float32)]
    broadcast_in_dim x16, local copies, waits for them, and re-layouts: 64.8 us -> 31.5 us  [block_terms(): mask = jnp.repeat(keep[:, :, column], BLK, axis=0)]
    dot_general x16, matrix products: 102 us -> 80.7 us  [block_terms(): real_imag = jnp.dot(masked[0], right[1], preferred_element_type=jnp.float32)]
    dot_general x16, matrix products: 102 us -> 84.5 us  [block_terms(): imag_real = jnp.dot(masked[1], right[0], preferred_element_type=jnp.float32)]
  transfers between devices with their start and end apart: 2 -> 2, of which waited for: 2 -> 1; matrix products, arithmetic and copies ran while one was open for 16% -> 24% of each run, Pallas kernels for 0% -> 0%
where the time goes in v1:
time: 951 us; the launch traced here: 942 us
  matrix products  326 us (34%)
  other arithmetic  205 us (22%)
  blocking collectives  205 us (22%)
  waiting for transfers between devices  129 us (14%)
  local copies, waits for them, and re-layouts  58.1 us (6%)
  between operations  15.7 us (2%)
    psum x1, blocking collectives, shards(): kept_total = lax.psum(jnp.sum(kept_count).reshape(1), ('row', 'col'))  205 us
    select_n x6, other arithmetic, block_terms(): masked = jnp.where(mask[None], a_piece, jnp.zeros((), jnp.bfloat16))  176 us
    all_gather x1, waiting for transfers between devices, shards(): lax.all_gather(b_eff, 'row', axis=1, tiled=True)  129 us
    dot_general x16, matrix products, block_terms(): real_real = jnp.dot(masked[0], right[0], preferred_element_type=jnp.float32)  92.2 us
    dot_general x16, matrix products, block_terms(): imag_real = jnp.dot(masked[1], right[0], preferred_element_type=jnp.float32)  84.5 us
    dot_general x16, matrix products, block_terms(): real_imag = jnp.dot(masked[0], right[1], preferred_element_type=jnp.float32)  80.7 us
    dot_general x16, matrix products, block_terms(): imag_imag = jnp.dot(masked[1], right[1], preferred_element_type=jnp.float32)  68.5 us
    broadcast_in_dim x16, local copies, waits for them, and re-layouts, block_terms(): mask = jnp.repeat(keep[:, :, column], BLK, axis=0)  31.5 us
  transfers between devices with their start and end apart: 2, of which 1 were waited for; matrix products, arithmetic and copies ran while one was open for 24% of the time, Pallas kernels for 0%

profile of v1, /device:TPU:0, one launch (start us, length us, event | category | flops | bytes accessed | tf_op | source)
XLA Modules:
  0.0 942.4 jit_solution(15675251617840426544)
XLA Ops:
  8.2 4.5 broadcast_in_dim.218
  18.7 4.5 broadcast_in_dim.215
  25.3 8.5 broadcast_multiply_fusion.1
  40.7 205.5 %psum.7 = s32[1]{0:T(128)} all-reduce(s32[1]{0:T(128)} %bitcast.131), channel_id=1, replica_groups=mesh['kpt'=4,'row'=4,'col'=2] {'row','col'}, use_global_device_ids=true, to_apply=%region_2.3 | all-reduce | flops 1 | bytes 8 | tf_op jit(solution)/shard_map/psum | solution.py:68
  248.2 20.4 %broadcast_select_fusion.15 = bf16[2,1024,4096]{2,1,0:T(8,128)(2,1)} fusion(pred[1024,4096]{1,0:T(8,128)(4,1)S(1)} %bitcast.601, bf16[2,1024,2048]{2,1,0:T(8,128)(2,1)} %broadcast_multiply_fusion.1, bf16[2,1024,2048]{2,1,0:T(8,128)(2,1)} %collective-permute-done, pred[]{:T(512)S(6)} %eq.3), kind=kLoop, calls=%fused_computation.16 | loop fusion | flops 83886080 | bytes 37748736 | tf_op jit(solution)/shard_map/jit(_where)/select_n | solution.py:28
  274.5 31.1 %broadcast_select_fusion.4 = (bf16[2,1024,4096]{2,1,0:T(8,128)(2,1)}, bf16[2,1024,4096]{2,1,0:T(8,128)(2,1)}, bf16[2,1024,4096]{2,1,0:T(8,128)(2,1)}) fusion(pred[1024,4096]{1,0:T(8,128)(4,1)S(1)} %bitcast.587, bf16[2,1024,2048]{2,1,0:T(8,128)(2,1)} %broadcast_multiply_fusion.1, bf16[2,1024,2048]{2,1,0:T(8,128)(2,1)} %collective-permute-done, pred[]{:T(512)S(6)} %eq.3, ...), kind=kLoop, calls=%fused_computation.5 | loop fusion | flops 100663296 | bytes 79691776 | tf_op jit(solution)/shard_map/jit(_where)/select_n | solution.py:28
  311.5 31.3 %broadcast_select_fusion.3 = (bf16[2,1024,4096]{2,1,0:T(8,128)(2,1)}, bf16[2,1024,4096]{2,1,0:T(8,128)(2,1)}, bf16[2,1024,4096]{2,1,0:T(8,128)(2,1)}) fusion(pred[1024,4096]{1,0:T(8,128)(4,1)S(1)} %bitcast.588, bf16[2,1024,2048]{2,1,0:T(8,128)(2,1)} %broadcast_multiply_fusion.1, bf16[2,1024,2048]{2,1,0:T(8,128)(2,1)} %collective-permute-done, pred[]{:T(512)S(6)} %eq.3, ...), kind=kLoop, calls=%fused_computation.4 | loop fusion | flops 100663296 | bytes 79691776 | tf_op jit(solution)/shard_map/jit(_where)/select_n | solution.py:28
  348.8 31.1 %broadcast_select_fusion.2 = (bf16[2,1024,4096]{2,1,0:T(8,128)(2,1)}, bf16[2,1024,4096]{2,1,0:T(8,128)(2,1)}, bf16[2,1024,4096]{2,1,0:T(8,128)(2,1)}) fusion(pred[1024,4096]{1,0:T(8,128)(4,1)S(1)} %bitcast.589, bf16[2,1024,2048]{2,1,0:T(8,128)(2,1)} %broadcast_multiply_fusion.1, bf16[2,1024,2048]{2,1,0:T(8,128)(2,1)} %collective-permute-done, pred[]{:T(512)S(6)} %eq.3, ...), kind=kLoop, calls=%fused_computation.3 | loop fusion | flops 100663296 | bytes 79691776 | tf_op jit(solution)/shard_map/jit(_where)/select_n | solution.py:28
  385.7 31.1 %broadcast_select_fusion.1 = (bf16[2,1024,4096]{2,1,0:T(8,128)(2,1)}, bf16[2,1024,4096]{2,1,0:T(8,128)(2,1)}, bf16[2,1024,4096]{2,1,0:T(8,128)(2,1)}) fusion(pred[1024,4096]{1,0:T(8,128)(4,1)S(1)} %bitcast.590, bf16[2,1024,2048]{2,1,0:T(8,128)(2,1)} %broadcast_multiply_fusion.1, bf16[2,1024,2048]{2,1,0:T(8,128)(2,1)} %collective-permute-done, pred[]{:T(512)S(6)} %eq.3, ...), kind=kLoop, calls=%fused_computation.2 | loop fusion | flops 100663296 | bytes 79691776 | tf_op jit(solution)/shard_map/jit(_where)/select_n | solution.py:28
  422.7 31.4 %broadcast_select_fusion = (bf16[2,1024,4096]{2,1,0:T(8,128)(2,1)}, bf16[2,1024,4096]{2,1,0:T(8,128)(2,1)}, bf16[2,1024,4096]{2,1,0:T(8,128)(2,1)}) fusion(pred[1024,4096]{1,0:T(8,128)(4,1)S(1)} %bitcast.584, bf16[2,1024,2048]{2,1,0:T(8,128)(2,1)} %broadcast_multiply_fusion.1, bf16[2,1024,2048]{2,1,0:T(8,128)(2,1)} %collective-permute-done, pred[]{:T(512)S(6)} %eq.3, ...), kind=kLoop, calls=%fused_computation.1 | loop fusion | flops 100663296 | bytes 79691776 | tf_op jit(solution)/shard_map/jit(_where)/select_n | solution.py:28
  454.1 128.9 %all-gather.2.cloned.1.call-done = bf16[2,4096,2048]{2,1,0:T(8,128)(2,1)} async-done(((bf16[2,1024,2048]{2,1,0:T(8,128)(2,1)}), bf16[2,4096,2048]{2,1,0:T(8,128)(2,1)}) %all-gather.2.cloned.1.call-update) | async-done | bytes 33554448 | tf_op jit(solution)/shard_map/all_gather | solution.py:65
  583.1 6.7 fusion.2
  589.7 6.7 fusion.3
  600.6 4.3 fusion.159
  605.7 7.1 fusion.6
  617.0 6.8 fusion.158
  623.9 6.7 fusion.157
  639.7 4.3 fusion.156
  644.0 6.8 fusion.155
  651.6 4.3 fusion.14
  660.0 6.7 fusion.154
  666.7 6.7 fusion.153
  682.5 4.7 fusion.152
  687.2 6.7 fusion.151
  703.0 6.7 fusion.150
  709.7 6.7 fusion.149
  717.2 4.3 fusion.26
  725.6 4.3 fusion.148
  729.9 6.7 fusion.147
  745.7 6.9 fusion.146
  752.6 6.7 fusion.145
  768.4 4.3 fusion.144
  772.7 6.7 fusion.143
  780.2 4.5 fusion.38
  788.9 6.7 fusion.142
  795.6 6.7 fusion.141
  811.4 4.4 fusion.140
  815.9 6.7 fusion.139
  835.9 4.3 fusion.137
  841.0 7.3 fusion.50
  856.6 4.3 fusion.135
  861.8 7.1 fusion.54
  873.1 4.5 fusion.134
  877.6 4.3 fusion.133
  882.7 7.1 fusion.58
  898.2 4.3 fusion.131
  903.3 7.3 fusion.62
  923.8 11.6 %copy.28 = bf16[2,1024,2048]{2,1,0:T(8,128)(2,1)} copy(bf16[2,1024,2048]{1,2,0:T(8,128)(2,1)} %maximum_dynamic-update-slice_fusion) | data formatting | bytes 16777216
  (234 shorter events, 176.5 us)
Async XLA Ops:
  7.2 575.9 %all-gather.2.cloned.1.call-start = ((), (), s32[]{:S(2)}) async-start(), calls=%async_computation | async-start | bytes 41943040 | tf_op jit(solution)/shard_map/all_gather | solution.py:65
  7.2 7.6 copy-start
  18.7 18.1 %copy-start.2 = (s32[8,16]{1,0:T(8,128)S(1)}, s32[8,16]{1,0:T(8,128)}, u32[]{:S(2)}) copy-start(s32[8,16]{1,0:T(8,128)} %param.9) | copy-start | bytes 1540
  18.7 18.9 %copy-start.1 = (s32[32,32]{1,0:T(8,128)S(1)}, s32[32,32]{1,0:T(8,128)}, u32[]{:S(2)}) copy-start(s32[32,32]{1,0:T(8,128)} %param.8) | copy-start | bytes 12292
  33.8 212.4 %collective-permute-start = (bf16[2,1024,2048]{2,1,0:T(8,128)(2,1)}, bf16[2,1024,2048]{2,1,0:T(8,128)(2,1)}, u32[]{:S(2)}, u32[]{:S(2)}) collective-permute-start(bf16[2,1024,2048]{2,1,0:T(8,128)(2,1)} %broadcast_multiply_fusion.1), channel_id=1, source_target_pairs={{0,1},{1,0},{2,3},{3,2},{4,5},{5,4},{6,7},{7,6},{8,9},{9,8},{10,11... | collective-permute-start | bytes 25165832 | tf_op jit(solution)/shard_map/ppermute | solution.py:58
  583.0 13.4 %slice-start = ((s8[16777216]{0:T(1024)(128)(4,1)}), s8[4194304]{0:T(1024)(128)(4,1)S(1)}, s32[]{:S(2)}) async-start(s8[16777216]{0:T(1024)(128)(4,1)} %bitcast.582), calls=%async_computation.1 | async-start | bytes 8388608
  583.1 13.4 %slice-start.1 = ((s8[16777216]{0:T(1024)(128)(4,1)}), s8[4194304]{0:T(1024)(128)(4,1)S(1)}, s32[]{:S(2)}) async-start(s8[16777216]{0:T(1024)(128)(4,1)} %bitcast.582), calls=%async_computation.2 | async-start | bytes 8388608
  600.6 12.2 %slice-start.60 = ((s8[16777216]{0:T(1024)(128)(4,1)}), s8[4194304]{0:T(1024)(128)(4,1)S(1)}, s32[]{:S(2)}) async-start(s8[16777216]{0:T(1024)(128)(4,1)} %bitcast.632), calls=%async_computation.61 | async-start | bytes 8388608
  600.6 12.2 %slice-start.61 = ((s8[16777216]{0:T(1024)(128)(4,1)}), s8[4194304]{0:T(1024)(128)(4,1)S(1)}, s32[]{:S(2)}) async-start(s8[16777216]{0:T(1024)(128)(4,1)} %bitcast.632), calls=%async_computation.62 | async-start | bytes 8388608
  604.9 8.0 slice-start.62
  617.0 14.4 %slice-start.56 = ((s8[16777216]{0:T(1024)(128)(4,1)}), s8[4194304]{0:T(1024)(128)(4,1)S(1)}, s32[]{:S(2)}) async-start(s8[16777216]{0:T(1024)(128)(4,1)} %bitcast.630), calls=%async_computation.57 | async-start | bytes 8388608
  617.0 14.4 %slice-start.57 = ((s8[16777216]{0:T(1024)(128)(4,1)}), s8[4194304]{0:T(1024)(128)(4,1)S(1)}, s32[]{:S(2)}) async-start(s8[16777216]{0:T(1024)(128)(4,1)} %bitcast.630), calls=%async_computation.58 | async-start | bytes 8388608
  639.6 11.9 %slice-start.52 = ((s8[16777216]{0:T(1024)(128)(4,1)}), s8[4194304]{0:T(1024)(128)(4,1)S(1)}, s32[]{:S(2)}) async-start(s8[16777216]{0:T(1024)(128)(4,1)} %bitcast.628), calls=%async_computation.53 | async-start | bytes 8388608
  639.7 11.9 %slice-start.53 = ((s8[16777216]{0:T(1024)(128)(4,1)}), s8[4194304]{0:T(1024)(128)(4,1)S(1)}, s32[]{:S(2)}) async-start(s8[16777216]{0:T(1024)(128)(4,1)} %bitcast.628), calls=%async_computation.54 | async-start | bytes 8388608
  643.9 7.6 slice-start.54
  644.0 7.6 slice-start.55
  660.0 14.2 %slice-start.48 = ((s8[16777216]{0:T(1024)(128)(4,1)}), s8[4194304]{0:T(1024)(128)(4,1)S(1)}, s32[]{:S(2)}) async-start(s8[16777216]{0:T(1024)(128)(4,1)} %bitcast.626), calls=%async_computation.49 | async-start | bytes 8388608
  660.0 14.2 %slice-start.49 = ((s8[16777216]{0:T(1024)(128)(4,1)}), s8[4194304]{0:T(1024)(128)(4,1)S(1)}, s32[]{:S(2)}) async-start(s8[16777216]{0:T(1024)(128)(4,1)} %bitcast.626), calls=%async_computation.50 | async-start | bytes 8388608
  682.5 12.2 %slice-start.44 = ((s8[16777216]{0:T(1024)(128)(4,1)}), s8[4194304]{0:T(1024)(128)(4,1)S(1)}, s32[]{:S(2)}) async-start(s8[16777216]{0:T(1024)(128)(4,1)} %bitcast.624), calls=%async_computation.45 | async-start | bytes 8388608
  682.5 12.2 %slice-start.45 = ((s8[16777216]{0:T(1024)(128)(4,1)}), s8[4194304]{0:T(1024)(128)(4,1)S(1)}, s32[]{:S(2)}) async-start(s8[16777216]{0:T(1024)(128)(4,1)} %bitcast.624), calls=%async_computation.46 | async-start | bytes 8388608
  703.0 14.2 %slice-start.40 = ((s8[16777216]{0:T(1024)(128)(4,1)}), s8[4194304]{0:T(1024)(128)(4,1)S(1)}, s32[]{:S(2)}) async-start(s8[16777216]{0:T(1024)(128)(4,1)} %bitcast.622), calls=%async_computation.41 | async-start | bytes 8388608
  703.0 14.2 %slice-start.41 = ((s8[16777216]{0:T(1024)(128)(4,1)}), s8[4194304]{0:T(1024)(128)(4,1)S(1)}, s32[]{:S(2)}) async-start(s8[16777216]{0:T(1024)(128)(4,1)} %bitcast.622), calls=%async_computation.42 | async-start | bytes 8388608
  725.6 11.8 %slice-start.36 = ((s8[16777216]{0:T(1024)(128)(4,1)}), s8[4194304]{0:T(1024)(128)(4,1)S(1)}, s32[]{:S(2)}) async-start(s8[16777216]{0:T(1024)(128)(4,1)} %bitcast.620), calls=%async_computation.37 | async-start | bytes 8388608
  725.6 11.8 %slice-start.37 = ((s8[16777216]{0:T(1024)(128)(4,1)}), s8[4194304]{0:T(1024)(128)(4,1)S(1)}, s32[]{:S(2)}) async-start(s8[16777216]{0:T(1024)(128)(4,1)} %bitcast.620), calls=%async_computation.38 | async-start | bytes 8388608
  745.7 14.4 %slice-start.32 = ((s8[16777216]{0:T(1024)(128)(4,1)}), s8[4194304]{0:T(1024)(128)(4,1)S(1)}, s32[]{:S(2)}) async-start(s8[16777216]{0:T(1024)(128)(4,1)} %bitcast.618), calls=%async_computation.33 | async-start | bytes 8388608
  745.7 14.4 %slice-start.33 = ((s8[16777216]{0:T(1024)(128)(4,1)}), s8[4194304]{0:T(1024)(128)(4,1)S(1)}, s32[]{:S(2)}) async-start(s8[16777216]{0:T(1024)(128)(4,1)} %bitcast.618), calls=%async_computation.34 | async-start | bytes 8388608
  768.4 11.9 %slice-start.28 = ((s8[16777216]{0:T(1024)(128)(4,1)}), s8[4194304]{0:T(1024)(128)(4,1)S(1)}, s32[]{:S(2)}) async-start(s8[16777216]{0:T(1024)(128)(4,1)} %bitcast.616), calls=%async_computation.29 | async-start | bytes 8388608
  768.4 11.8 %slice-start.29 = ((s8[16777216]{0:T(1024)(128)(4,1)}), s8[4194304]{0:T(1024)(128)(4,1)S(1)}, s32[]{:S(2)}) async-start(s8[16777216]{0:T(1024)(128)(4,1)} %bitcast.616), calls=%async_computation.30 | async-start | bytes 8388608
  772.7 7.6 slice-start.30
  788.9 14.2 %slice-start.24 = ((s8[16777216]{0:T(1024)(128)(4,1)}), s8[4194304]{0:T(1024)(128)(4,1)S(1)}, s32[]{:S(2)}) async-start(s8[16777216]{0:T(1024)(128)(4,1)} %bitcast.614), calls=%async_computation.25 | async-start | bytes 8388608
  788.9 14.2 %slice-start.25 = ((s8[16777216]{0:T(1024)(128)(4,1)}), s8[4194304]{0:T(1024)(128)(4,1)S(1)}, s32[]{:S(2)}) async-start(s8[16777216]{0:T(1024)(128)(4,1)} %bitcast.614), calls=%async_computation.26 | async-start | bytes 8388608
  795.6 7.6 slice-start.26
  811.4 12.0 %slice-start.4 = ((s8[16777216]{0:T(1024)(128)(4,1)}), s8[4194304]{0:T(1024)(128)(4,1)S(1)}, s32[]{:S(2)}) async-start(s8[16777216]{0:T(1024)(128)(4,1)} %bitcast.604), calls=%async_computation.5 | async-start | bytes 8388608
  811.4 12.0 %slice-start.5 = ((s8[16777216]{0:T(1024)(128)(4,1)}), s8[4194304]{0:T(1024)(128)(4,1)S(1)}, s32[]{:S(2)}) async-start(s8[16777216]{0:T(1024)(128)(4,1)} %bitcast.604), calls=%async_computation.6 | async-start | bytes 8388608
  815.9 7.6 slice-start.6
  815.9 7.6 slice-start.7
  835.8 12.5 %slice-start.8 = ((s8[16777216]{0:T(1024)(128)(4,1)}), s8[4194304]{0:T(1024)(128)(4,1)S(1)}, s32[]{:S(2)}) async-start(s8[16777216]{0:T(1024)(128)(4,1)} %bitcast.606), calls=%async_computation.9 | async-start | bytes 8388608
  835.8 12.5 %slice-start.9 = ((s8[16777216]{0:T(1024)(128)(4,1)}), s8[4194304]{0:T(1024)(128)(4,1)S(1)}, s32[]{:S(2)}) async-start(s8[16777216]{0:T(1024)(128)(4,1)} %bitcast.606), calls=%async_computation.10 | async-start | bytes 8388608
  840.1 8.2 slice-start.10
  856.6 12.3 %slice-start.12 = ((s8[16777216]{0:T(1024)(128)(4,1)}), s8[4194304]{0:T(1024)(128)(4,1)S(1)}, s32[]{:S(2)}) async-start(s8[16777216]{0:T(1024)(128)(4,1)} %bitcast.608), calls=%async_computation.13 | async-start | bytes 8388608
  856.6 12.3 %slice-start.13 = ((s8[16777216]{0:T(1024)(128)(4,1)}), s8[4194304]{0:T(1024)(128)(4,1)S(1)}, s32[]{:S(2)}) async-start(s8[16777216]{0:T(1024)(128)(4,1)} %bitcast.608), calls=%async_computation.14 | async-start | bytes 8388608
  860.9 8.0 slice-start.14
  877.6 12.3 %slice-start.16 = ((s8[16777216]{0:T(1024)(128)(4,1)}), s8[4194304]{0:T(1024)(128)(4,1)S(1)}, s32[]{:S(2)}) async-start(s8[16777216]{0:T(1024)(128)(4,1)} %bitcast.610), calls=%async_computation.17 | async-start | bytes 8388608
  877.6 12.3 %slice-start.17 = ((s8[16777216]{0:T(1024)(128)(4,1)}), s8[4194304]{0:T(1024)(128)(4,1)S(1)}, s32[]{:S(2)}) async-start(s8[16777216]{0:T(1024)(128)(4,1)} %bitcast.610), calls=%async_computation.18 | async-start | bytes 8388608
  881.9 8.0 slice-start.18
  898.1 12.4 %slice-start.20 = ((s8[16777216]{0:T(1024)(128)(4,1)}), s8[4194304]{0:T(1024)(128)(4,1)S(1)}, s32[]{:S(2)}) async-start(s8[16777216]{0:T(1024)(128)(4,1)} %bitcast.612), calls=%async_computation.21 | async-start | bytes 8388608
  898.2 12.4 %slice-start.21 = ((s8[16777216]{0:T(1024)(128)(4,1)}), s8[4194304]{0:T(1024)(128)(4,1)S(1)}, s32[]{:S(2)}) async-start(s8[16777216]{0:T(1024)(128)(4,1)} %bitcast.612), calls=%async_computation.22 | async-start | bytes 8388608
  902.4 8.1 slice-start.22
  (21 other events, 154.7 us)
Sparse Core Ops, SparseCore 0:
  18.7 564.2 all-gather.1
